TPU v7x, 128 devices: a whole 4x4x4 slice. The times are simulated.
128 devices in a mesh: lat: 8 (over x, core), lev: 16 (over y, z).
Axes of the slice: x: 4, y: 4, z: 4, core: 2. Of those that a mesh axis runs over, the one named last changes fastest.
Arguments:
- spectral: float32 [2, 128, 256, 256], P(None, 'lev', 'lat'), may hold values from -6 to 6
- background: bfloat16 [384, 768, 128], P('lat', 'lev'), may hold values from -6 to 6
- columns: int32 [128, 2048], P(('lat', 'lev')), may hold values from 0 to 2303
- counts: int32 [128], P(('lat', 'lev')), may hold values from 1 to 2048, 131072 in all
- radiances: bfloat16 [128, 2048, 512], P(('lat', 'lev')), may hold values from -6 to 6
- used_pairs: int32 [128, 2048], P(('lat', 'lev')), may hold values from 1 to 256
- channel_weight: float32 [512], replicated, may hold values from 0.25 to 4
- weight_in: bfloat16 [128, 1024], replicated, may hold values from -0.5 to 0.5
- weight_mid: bfloat16 [1024, 1024], replicated, may hold values from -0.1875 to 0.1875
- weight_out: bfloat16 [1024, 512], replicated, may hold values from -0.1875 to 0.1875
Outputs:
- spectral_grad: float32 [2, 128, 256, 256], P(None, 'lev', 'lat')
- grid_grad: float32 [384, 768, 128], P('lat', 'lev')
Inputs may be any that keep to these rules, and one draw needn't show every extreme that they name: Entry [o, s] is the column of owner o's slot s inside o's region of 48 x 48 columns, numbered latitude-major; slots at or past counts[o] are unused. The counts sum to 131072, and the largest is exactly 2048. Block [o, s] uses channels 0 to 2 x used_pairs[o, s] - 1.
All inputs are finite; a program needn't handle non-finite values. No bound on the sum of `counts` on one device may be relied on, other than what follows from the above.
Results may differ from a plain program's by a relative error of at most 0.008.
Values may be sent and summed in bfloat16 or wider, within the bound.
No kernel may reach another device: no remote copies, remote signals or barrier semaphores. Data moves between devices by JAX's collectives and lax.ppermute only.
A program may use at most 128 MiB of HBM per device.

v0:
```python
import math
import jax
import jax.numpy as jnp
from jax import lax
from jax.sharding import PartitionSpec as P

M = 256
N = 256
NLAT = 384
NLON = 768
BLK_DEV = 1024
RESCALE_TOP = 2.0**60
RESCALE_BY = 2.0 ** (-60)
RESCALE_LOG = 60.0 * math.log(2.0)
HALF_LOG = 0.5 * math.log(0.5)


def shortened(shard):
    return jax.tree.map(lambda a: a.astype(jnp.bfloat16) if a.dtype == jnp.float32 else a, shard)


def legendre_table(orders, lat_total, degree_total):
    m_float = orders.astype(jnp.float32)
    lat_ids = jnp.arange(lat_total, dtype=jnp.float32)
    latitude = (0.5 - (lat_ids + 0.5) / lat_total) * jnp.pi
    sin_lat = jnp.sin(latitude)
    cos_lat = jnp.cos(latitude)
    order_ids = jnp.arange(1, degree_total, dtype=jnp.float32)
    log_steps = 0.5 * jnp.log((2.0 * order_ids + 1.0) / (2.0 * order_ids))
    log_norm = jnp.sum(
        jnp.where(order_ids[None, :] <= m_float[:, None], log_steps[None, :], 0.0), axis=1
    )
    log_start = HALF_LOG + log_norm[:, None] + m_float[:, None] * jnp.log(cos_lat)[None, :]

    def advance(recur_state, degree):
        previous, earlier, shifts = recur_state
        n_float = degree.astype(jnp.float32)
        on_diagonal = (n_float == m_float)[:, None]
        next_diag = (n_float == m_float + 1.0)[:, None]
        beyond = (n_float > m_float + 1.0)[:, None]
        factor_a = jnp.sqrt(
            jnp.maximum(4.0 * n_float * n_float - 1.0, 1.0)
            / jnp.maximum(n_float * n_float - m_float * m_float, 1.0)
        )
        lower = n_float - 1.0
        factor_b = jnp.sqrt(
            jnp.maximum(lower * lower - m_float * m_float, 0.0)
            / jnp.maximum(4.0 * lower * lower - 1.0, 1.0)
        )
        current = jnp.where(
            beyond,
            factor_a[:, None] * (sin_lat[None, :] * previous - factor_b[:, None] * earlier),
            0.0,
        )
        current = jnp.where(
            next_diag, jnp.sqrt(2.0 * m_float + 3.0)[:, None] * sin_lat[None, :] * previous, current
        )
        current = jnp.where(on_diagonal, 1.0, current)
        oversized = jnp.abs(current) > RESCALE_TOP
        current = jnp.where(oversized, current * RESCALE_BY, current)
        previous = jnp.where(oversized, previous * RESCALE_BY, previous)
        shifts = shifts + oversized.astype(jnp.float32)
        values = current * jnp.exp(log_start + shifts * RESCALE_LOG)
        return ((current, previous, shifts), values)

    zeros = jnp.zeros((orders.shape[0], lat_total), jnp.float32)
    _, legendre = lax.scan(
        advance, (zeros, zeros, zeros), jnp.arange(degree_total, dtype=jnp.int32), unroll=8
    )
    return legendre


def wave_table(wave_total, lon_total):
    wave_ids = jnp.arange(wave_total, dtype=jnp.int32)
    lon_ids = jnp.arange(lon_total, dtype=jnp.int32)
    phase = (wave_ids[:, None] * lon_ids[None, :] % lon_total).astype(jnp.float32) * (
        2.0 * math.pi / lon_total
    )
    weights = jnp.where(wave_ids == 0, 1.0, 2.0).astype(jnp.float32) / wave_total
    return jnp.stack([weights[:, None] * jnp.cos(phase), -weights[:, None] * jnp.sin(phase)])


def silu_slope(inputs):
    sigmoid_v = jax.nn.sigmoid(inputs)
    return sigmoid_v * (1.0 + inputs * (1.0 - sigmoid_v))


def radiance_pass(
    profiles, observed, pair_counts, usable, channel_weight, weight_in, weight_mid, weight_out
):
    pre_first = jnp.dot(profiles, weight_in, preferred_element_type=jnp.float32)
    act_first = jax.nn.silu(pre_first).astype(jnp.bfloat16)
    pre_second = jnp.dot(act_first, weight_mid, preferred_element_type=jnp.float32)
    act_second = jax.nn.silu(pre_second).astype(jnp.bfloat16)
    evolved = jnp.dot(act_second, weight_out, preferred_element_type=jnp.float32)
    channel_ids = jnp.arange(weight_out.shape[1], dtype=jnp.float32)
    active = (channel_ids[None, :] < 2.0 * pair_counts[:, None]) & usable[:, None]
    misfit = jnp.where(
        active, channel_weight[None, :] * (evolved - observed.astype(jnp.float32)), 0.0
    ).astype(jnp.bfloat16)
    back_second = (
        jnp.dot(misfit, weight_out.T, preferred_element_type=jnp.float32) * silu_slope(pre_second)
    ).astype(jnp.bfloat16)
    back_first = (
        jnp.dot(back_second, weight_mid.T, preferred_element_type=jnp.float32)
        * silu_slope(pre_first)
    ).astype(jnp.bfloat16)
    return jnp.dot(back_first, weight_in.T, preferred_element_type=jnp.float32).astype(jnp.bfloat16)


def route_out(profile_slots, observed_slots, pair_slots):
    arrived = (
        lax.all_to_all(profile_slots, ("lat", "lev"), split_axis=1, concat_axis=1, tiled=True),
        lax.all_to_all(observed_slots, ("lat", "lev"), split_axis=1, concat_axis=1, tiled=True),
        lax.all_to_all(pair_slots, ("lat", "lev"), split_axis=1, concat_axis=1, tiled=True),
    )
    return arrived


def route_back(reply):
    returned = lax.all_to_all(reply, ("lat", "lev"), split_axis=1, concat_axis=1, tiled=True)
    return returned


def dealt(
    profiles,
    observed,
    pair_counts,
    usable,
    counts,
    own_index,
    lat_count,
    lev_count,
    channel_weight,
    weight_in,
    weight_mid,
    weight_out,
):
    devices = lat_count * lev_count
    all_counts = lax.all_gather(counts, ("lat", "lev"), axis=0, tiled=True)
    start_ranks = jnp.cumsum(all_counts) - all_counts
    owner_ids = jnp.arange(devices, dtype=jnp.int32)
    own_start = jnp.sum(jnp.where(owner_ids == own_index, start_ranks, 0))
    lead_pos = own_start % devices
    capacity = profiles.shape[0]
    slot_count = (capacity + 2 * devices - 2) // devices

    def place(rows):
        keep = usable.reshape((capacity,) + (1,) * (rows.ndim - 1))
        masked = jnp.where(keep, rows, jnp.zeros((), rows.dtype))
        frame = jnp.zeros((slot_count * devices,) + rows.shape[1:], rows.dtype)
        frame = lax.dynamic_update_slice_in_dim(frame, masked, lead_pos, 0)
        return frame.reshape((slot_count, devices) + rows.shape[1:])

    arrived = route_out(place(profiles), place(observed), place(pair_counts.astype(jnp.bfloat16)))
    flat_profiles = arrived[0].reshape(slot_count * devices, -1)
    flat_observed = arrived[1].reshape(slot_count * devices, -1)
    flat_pairs = arrived[2].reshape(slot_count * devices)
    row_ids = jnp.arange(BLK_DEV, dtype=jnp.int32)
    my_ranks = own_index + devices * row_ids
    covers = start_ranks[None, :] <= my_ranks[:, None]
    source = jnp.sum(covers.astype(jnp.int32), axis=1) - 1
    source_start = jnp.max(jnp.where(covers, start_ranks[None, :], 0), axis=1)
    flat_pos = (row_ids - source_start // devices) * devices + source
    worker_grad = radiance_pass(
        jnp.take(flat_profiles, flat_pos, axis=0),
        jnp.take(flat_observed, flat_pos, axis=0),
        jnp.take(flat_pairs, flat_pos, axis=0).astype(jnp.float32),
        jnp.ones((BLK_DEV,), jnp.bool_),
        channel_weight,
        weight_in,
        weight_mid,
        weight_out,
    )
    slot_ids = jnp.arange(slot_count, dtype=jnp.int32)
    position = slot_ids[:, None] * devices + own_index - (start_ranks % devices)[None, :]
    returned = (position >= 0) & (position < all_counts[None, :])
    target = jnp.clip(start_ranks[None, :] // devices + slot_ids[:, None], 0, BLK_DEV - 1)
    reply = jnp.take(worker_grad, target.reshape(-1), axis=0).reshape(
        slot_count, devices, worker_grad.shape[1]
    )
    reply = jnp.where(returned[:, :, None], reply, jnp.zeros((), jnp.bfloat16))
    back_rows = route_back(reply).reshape(slot_count * devices, -1)
    mine = lax.dynamic_slice_in_dim(back_rows, lead_pos, capacity, 0)
    return jnp.where(usable[:, None], mine, jnp.zeros((), jnp.bfloat16))


def per_device(
    spectral,
    background,
    columns,
    counts,
    radiances,
    used_pairs,
    channel_weight,
    weight_in,
    weight_mid,
    weight_out,
):
    highest = lax.Precision.HIGHEST
    lat_count = lax.axis_size("lat")
    lev_count = lax.axis_size("lev")
    lat_index = lax.axis_index("lat")
    lev_index = lax.axis_index("lev")
    own_index = lat_index * lev_count + lev_index
    waves_local = spectral.shape[2]
    orders = lat_index * waves_local + jnp.arange(waves_local, dtype=jnp.int32)
    legendre = legendre_table(orders, NLAT, N)
    fourier = jnp.einsum("nmj,clmn->clmj", legendre, spectral, precision=highest)
    fourier = lax.all_to_all(fourier, "lat", split_axis=3, concat_axis=2, tiled=True)
    dft_table = wave_table(M, NLON)
    increment = jnp.einsum("clmj,cmx->jlx", fourier, dft_table, precision=highest)
    increment = lax.all_to_all(increment, "lev", split_axis=2, concat_axis=1, tiled=True)
    increment = jnp.transpose(increment, (0, 2, 1))
    grid_state = (background.astype(jnp.float32) + increment).astype(jnp.bfloat16)
    band_rows = grid_state.shape[0]
    tile_cols = grid_state.shape[1]
    cell_rows = grid_state.reshape(band_rows * tile_cols, grid_state.shape[2])
    local_cols = columns[0]
    profiles = jnp.take(cell_rows, local_cols, axis=0)
    capacity = local_cols.shape[0]
    usable = jnp.arange(capacity, dtype=jnp.int32) < counts[0]
    observed = radiances[0]
    pair_counts = used_pairs[0].astype(jnp.float32)
    block_grad = dealt(
        profiles,
        observed,
        pair_counts,
        usable,
        counts,
        own_index,
        lat_count,
        lev_count,
        channel_weight,
        weight_in,
        weight_mid,
        weight_out,
    )
    grid_grad = (
        jnp.zeros(cell_rows.shape, jnp.float32).at[local_cols].add(block_grad.astype(jnp.float32))
    )
    grid_grad = grid_grad.reshape(band_rows, tile_cols, cell_rows.shape[1])
    grad_rows = lax.all_to_all(
        jnp.transpose(grid_grad, (0, 2, 1)).astype(jnp.bfloat16),
        "lev",
        split_axis=1,
        concat_axis=2,
        tiled=True,
    ).astype(jnp.float32)
    coeff_grad = jnp.einsum("jlx,cmx->clmj", grad_rows, dft_table, precision=highest)
    coeff_grad = lax.all_to_all(
        shortened(coeff_grad), "lat", split_axis=2, concat_axis=3, tiled=True
    ).astype(coeff_grad.dtype)
    spectral_grad = jnp.einsum("nmj,clmj->clmn", legendre, coeff_grad, precision=highest)
    return (spectral_grad, grid_grad)


def solution(mesh):
    in_specs = (
        P(None, "lev", "lat", None),
        P("lat", "lev", None),
        P(("lat", "lev"), None),
        P(("lat", "lev")),
        P(("lat", "lev"), None, None),
        P(("lat", "lev"), None),
        P(),
        P(),
        P(),
        P(),
    )
    out_specs = (P(None, "lev", "lat", None), P("lat", "lev", None))
    return jax.shard_map(
        per_device, mesh=mesh, in_specs=in_specs, out_specs=out_specs, check_vma=False
    )
```

profile of v0, /device:TPU:1, one launch (start us, length us, event | category | flops | bytes accessed | tf_op | source)
XLA Modules:
  0.0 645.3 jit_solution(7367198378319178831)
XLA Ops:
  1.0 258.0 %while.23 = (s32[]{:T(128)}, f32[32,384]{1,0:T(8,128)S(1)}, f32[32,384]{1,0:T(8,128)S(1)}, f32[32,384]{1,0:T(8,128)S(1)}, f32[32,8,32,384]{3,2,1,0:T(8,128)}, /*...) while((s32[]{:T(128)}, f32[32,384]{1,0:T(8,128)S(1)}, ...), condition=%wide.region_6.7_spmd.clone.clone.clone.clone, body=%wide.region_5.6_spmd.clone.clone.clone.clone.sunk | while | flops 3778274 | bytes 3127550 | solution.py:67
  259.0 14.5 %fusion.88 = f32[2,8,32,384]{3,1,0,2:T(8,128)S(1)} fusion(f32[256,32,384]{2,1,0:T(8,128)} %bitcast.226, f32[2,8,32,256]{3,2,1,0:T(8,128)S(1)} %copy-done.6), kind=kOutput, calls=%fused_computation.199 | convolution fusion | flops 603979776 | bytes 13893632
  279.3 5.8 all-to-all-start.1
  285.9 69.5 %all-reduce = s32[128]{0:T(128)S(1)} all-reduce(s32[128]{0:T(128)S(1)} %dynamic-update-slice), channel_id=1, replica_groups=mesh['lat'=8,'lev'=16] {'lat','lev'}, use_global_device_ids=true, to_apply=%add | all-reduce | flops 128 | bytes 1024
  359.9 4.1 sine_multiply_fusion
  364.0 5.0 all-to-all-start
  373.2 3.8 reshape.979
  377.0 5.4 copy.208
  385.5 3.7 convolution_bitcast_fusion
  391.5 5.1 reshape.980
  396.6 7.6 %all-to-all-start.2 = ((f32[16,1,18432]{2,1,0:T(1,128)}), f32[16,1,18432]{2,1,0:T(1,128)S(1)}, u32[]{:S(2)}, u32[]{:S(2)}) async-start(f32[16,1,18432]{2,1,0:T(1,128)} %reshape.980), calls=%async_computation.2 | async-start | bytes 2359296 | tf_op jit(solution)/shard_map/all_to_all | solution.py:213
  408.5 11.3 %dynamic_update_slice.19 = bf16[2176,512]{1,0:T(8,128)(2,1)} dynamic-update-slice(bf16[2176,512]{1,0:T(8,128)(2,1)} %broadcast_in_dim.596, bf16[2048,512]{1,0:T(8,128)(2,1)} %bitcast_select_fusion, s32[]{:T(128)S(6)} %select_n.488, s32[]{:T(128)} %constant.254.clone.1) | dynamic-update-slice | bytes 4194308 | tf_op jit(solution)/shard_map/dynamic_update_slice | solution.py:152
  419.7 4.6 copy.170
  424.9 10.1 %all-to-all-start.4 = ((bf16[17,128,512]{2,0,1:T(8,128)(2,1)}), bf16[17,128,512]{2,0,1:T(8,128)(2,1)}, u32[]{:S(2)}, u32[]{:S(2)}) async-start(bf16[17,128,512]{2,0,1:T(8,128)(2,1)} %copy.170), calls=%async_computation.4 | async-start | bytes 6291456 | tf_op jit(solution)/shard_map/all_to_all | solution.py:114
  435.7 4.8 reduce.6
  444.1 5.1 copy.166
  453.8 6.2 gather_fusion.1
  466.8 8.5 %all-to-all-done.4 = bf16[17,128,512]{2,0,1:T(8,128)(2,1)} async-done(((bf16[17,128,512]{2,0,1:T(8,128)(2,1)}), bf16[17,128,512]{2,0,1:T(8,128)(2,1)}, u32[]{:S(2)}, u32[]{:S(2)}) %all-to-all-start.4) | async-done | bytes 2228256 | tf_op jit(solution)/shard_map/all_to_all | solution.py:114
  475.4 5.3 all-to-all-start.3
  482.0 6.8 %gather_fusion = bf16[1024]{0:T(1024)(128)(2,1)S(1)} fusion(bf16[2176]{0:T(1024)(128)(2,1)S(1)} %bitcast.224, s32[1024]{0:T(1024)S(1)} %broadcast_clamp_fusion.1), kind=kCustom, calls=%fused_computation | custom fusion | bytes 8192 | tf_op jit(solution)/shard_map/jit(_take)/gather | solution.py:168
  489.6 4.0 copy.171
  493.6 7.0 %gather_fusion.3 = bf16[1024,512]{1,0:T(8,128)(2,1)} fusion(bf16[2176,512]{1,0:T(8,128)(2,1)} %bitcast.225, s32[1024]{0:T(1024)S(1)} %broadcast_clamp_fusion.1), kind=kCustom, calls=%fused_computation.3 | custom fusion | bytes 2101248 | tf_op jit(solution)/shard_map/jit(_take)/gather | solution.py:167
  505.7 4.3 fusion.85
  510.0 8.8 %multiply_convert_fusion.1 = bf16[1024,1024]{1,0:T(8,128)(2,1)} fusion(f32[1024,1024]{1,0:T(8,128)} %fusion.85, bf16[1024,512]{1,0:T(8,128)(2,1)} %param.21, bf16[1024,512]{1,0:T(8,128)(2,1)S(1)} %copy-done.3, f32[512]{0:T(512)S(1)} %copy-done.16, f32[1024]{0:T(1024)S(1)} %get-tuple-element.400, pred[1024]{0:T(1024)(128)(4,1)S(1)} %get-tuple-element.401), kind=kOutput, calls=%fused_computation.185 | convolution fusion | flops 2165833728 | bytes 8395776 | tf_op jit(solution)/shard_map/dot_general | solution.py:102
  518.9 6.0 fusion.97
  524.9 4.8 gather_fusion.4
  531.6 26.2 %all_to_all.96 = bf16[17,128,128]{2,0,1:T(8,128)(2,1)S(1)} all-to-all(bf16[17,128,128]{2,0,1:T(8,128)(2,1)S(1)} %fusion.108), channel_id=1, replica_groups=mesh['lat'=8,'lev'=16] {'lat','lev'}, dimensions={1} | all-to-all | bytes 1114112 | tf_op jit(solution)/shard_map/all_to_all | solution.py:121
  558.7 12.2 %scatter_custom_fusion = f32[2304,128]{1,0:T(8,128)S(1)} fusion(s32[2048]{0:T(1024)} %bitcast.249, f32[]{:T(128)} %constant.260.clone.1, bf16[2176,128]{1,0:T(8,128)(2,1)} %bitcast.245, s32[]{:T(128)S(6)} %select_n.488, s32[]{:T(128)} %constant.254.clone.1, pred[2048]{0:T(1024)(128)(4,1)S(1)} %copy-done.12, bf16[]{:T(256)} %constant.276.clone.1), kind=kCustom, calls=%fused_computation.208 | custom fusion | flops 786432 | bytes 1707524 | tf_op jit(solution)/shard_map/scatter-add | solution.py:240
  574.7 4.2 reshape.982
  578.8 15.5 %all_to_all.97 = bf16[16,2,9216]{2,1,0:T(2,128)(2,1)} all-to-all(bf16[16,2,9216]{2,1,0:T(2,128)(2,1)} %reshape.982), channel_id=1, replica_groups=mesh['lat'=8,'lev'=16] {'lev'}, dimensions={0} | all-to-all | bytes 1179648 | tf_op jit(solution)/shard_map/all_to_all | solution.py:243
  610.5 13.3 %all_to_all.98 = bf16[8,2,12288]{2,1,0:T(2,128)(2,1)} all-to-all(bf16[8,2,12288]{2,1,0:T(2,128)(2,1)S(1)} %reshape.984), channel_id=1, replica_groups=mesh['lat'=8,'lev'=16] {'lat'}, dimensions={0} | all-to-all | bytes 786432 | tf_op jit(solution)/shard_map/all_to_all | solution.py:251
  630.4 13.3 %fusion.93 = f32[2,8,32,256]{3,1,0,2:T(8,128)S(1)} fusion(bf16[2,8,32,384]{3,1,0,2:T(8,128)(2,1)S(1)} %all_to_all.87, f32[256,32,384,1]{2,1,0,3:T(8,128)} %bitcast.227), kind=kOutput, calls=%fused_computation.202 | convolution fusion | flops 603979776 | bytes 13500416 | tf_op jit(solution)/shard_map/nmj,clmj->clmn/dot_general | solution.py:254
  (1201 shorter events, 170.8 us)
Async XLA Ops:
  0.6 505.0 %copy-start = (bf16[1024,1024]{1,0:T(8,128)(2,1)S(1)}, bf16[1024,1024]{1,0:T(8,128)(2,1)}, u32[]{:S(2)}) copy-start(bf16[1024,1024]{1,0:T(8,128)(2,1)} %param.20) | copy-start | bytes 6291460
  1.0 258.1 %copy-start.6 = (f32[2,8,32,256]{3,2,1,0:T(8,128)S(1)}, f32[2,8,32,256]{3,2,1,0:T(8,128)}, u32[]{:S(2)}) copy-start(f32[2,8,32,256]{3,2,1,0:T(8,128)} %param.12) | copy-start | bytes 1572868
  275.8 82.7 %copy-start.15 = (s32[1,2048]{1,0:T(1,128)S(1)}, s32[1,2048]{1,0:T(1,128)}, u32[]{:S(2)}) copy-start(s32[1,2048]{1,0:T(1,128)} %param.17) | copy-start | bytes 24580
  279.3 84.7 %all-to-all-start.1 = ((f32[8,1,24576]{2,1,0:T(1,128)}), f32[8,1,24576]{2,1,0:T(1,128)S(1)}, u32[]{:S(2)}, u32[]{:S(2)}) async-start(f32[8,1,24576]{2,1,0:T(1,128)} %reshape.978), calls=%async_computation.1 | async-start | bytes 1572864 | tf_op jit(solution)/shard_map/all_to_all | solution.py:210
  364.0 32.6 %all-to-all-start = ((bf16[17,128,1]{0,2,1:T(2,128)(2,1)}), bf16[17,128,1]{0,2,1:T(2,128)(2,1)S(1)}, u32[]{:S(2)}, u32[]{:S(2)}) async-start(bf16[17,128,1]{0,2,1:T(2,128)(2,1)} %copy.158), calls=%async_computation | async-start | bytes 131072 | tf_op jit(solution)/shard_map/all_to_all | solution.py:115
  396.6 28.3 %all-to-all-start.2 = ((f32[16,1,18432]{2,1,0:T(1,128)}), f32[16,1,18432]{2,1,0:T(1,128)S(1)}, u32[]{:S(2)}, u32[]{:S(2)}) async-start(f32[16,1,18432]{2,1,0:T(1,128)} %reshape.980), calls=%async_computation.2 | async-start | bytes 2359296 | tf_op jit(solution)/shard_map/all_to_all | solution.py:213
  404.2 55.8 %copy-start.11 = (pred[2048]{0:T(1024)(128)(4,1)}, pred[2048]{0:T(1024)(128)(4,1)S(1)}, u32[]{:S(2)}) copy-start(pred[2048]{0:T(1024)(128)(4,1)S(1)} %iota_compare_fusion.1) | copy-start | bytes 6148
  424.8 10.2 %copy-start.10 = (s32[1024]{0:T(1024)}, s32[1024]{0:T(1024)S(1)}, u32[]{:S(2)}) copy-start(s32[1024]{0:T(1024)S(1)} %get-tuple-element.361) | copy-start | bytes 12292
  424.8 10.2 %copy-start.9 = (s32[1024]{0:T(1024)}, s32[1024]{0:T(1024)S(1)}, u32[]{:S(2)}) copy-start(s32[1024]{0:T(1024)S(1)} %get-tuple-element.360) | copy-start | bytes 12292
  424.8 10.2 %copy-start.13 = (s32[1,2048]{1,0:T(1,128)S(1)}, s32[1,2048]{1,0:T(1,128)}, u32[]{:S(2)}) copy-start(s32[1,2048]{1,0:T(1,128)} %param.14) | copy-start | bytes 24580
  424.9 50.5 %all-to-all-start.4 = ((bf16[17,128,512]{2,0,1:T(8,128)(2,1)}), bf16[17,128,512]{2,0,1:T(8,128)(2,1)}, u32[]{:S(2)}, u32[]{:S(2)}) async-start(bf16[17,128,512]{2,0,1:T(8,128)(2,1)} %copy.170), calls=%async_computation.4 | async-start | bytes 6291456 | tf_op jit(solution)/shard_map/all_to_all | solution.py:114
  435.7 8.4 %copy-start.14 = (s32[2048,1]{0,1:T(1,128)}, s32[2048,1]{0,1:T(1,128)S(1)}, u32[]{:S(2)}) copy-start(s32[2048,1]{0,1:T(1,128)S(1)} %compare_select_fusion.2) | copy-start | bytes 24580
  449.2 3.2 copy-start.5
  475.4 25.3 %all-to-all-start.3 = ((bf16[17,128,128]{2,0,1:T(8,128)(2,1)}), bf16[17,128,128]{2,0,1:T(8,128)(2,1)S(1)}, u32[]{:S(2)}, u32[]{:S(2)}) async-start(bf16[17,128,128]{2,0,1:T(8,128)(2,1)} %copy.168), calls=%async_computation.3 | async-start | bytes 1572864 | tf_op jit(solution)/shard_map/all_to_all | solution.py:113
  505.7 4.4 copy-start.2
  505.7 4.4 copy-start.3
  505.7 4.3 copy-start.16
  510.0 8.8 %copy-start.7 = (bf16[128,1024]{1,0:T(8,128)(2,1)S(1)}, bf16[128,1024]{1,0:T(8,128)(2,1)}, u32[]{:S(2)}) copy-start(bf16[128,1024]{1,0:T(8,128)(2,1)} %param.19) | copy-start | bytes 786436
  518.9 6.0 copy-start.8
  529.7 29.0 %copy-start.12 = (pred[2048]{0:T(1024)(128)(4,1)S(1)}, pred[2048]{0:T(1024)(128)(4,1)}, u32[]{:S(2)}) copy-start(pred[2048]{0:T(1024)(128)(4,1)} %copy-done.11) | copy-start | bytes 6148
  571.0 23.3 %copy-start.1 = (f32[2304,128]{1,0:T(8,128)}, f32[2304,128]{1,0:T(8,128)S(1)}, u32[]{:S(2)}) copy-start(f32[2304,128]{1,0:T(8,128)S(1)} %scatter_custom_fusion) | copy-start | bytes 3538948
  597.6 6.4 copy-start.4
where the time goes:
time: 658 us; the launch traced here: 645 us
  local copies, waits for them, and re-layouts  170 us (26%)
  loops' own time  163 us (25%)
  blocking collectives  125 us (19%)
  other arithmetic  85.6 us (13%)
  matrix products  55.4 us (8%)
  starting transfers between devices  33.7 us (5%)
  waiting for transfers between devices  8.55 us (1%)
    another operation x1, loops' own time, legendre_table(): lax.scan(advance, (zeros, zeros, zeros), jnp.arange(degree_total, dtype=j...  163 us
    unnamed x1, blocking collectives  69.5 us
    while x224, other arithmetic  31.7 us
    unnamed x45, local copies, waits for them, and re-layouts  28.7 us
    all_to_all x1, blocking collectives, route_back(): lax.all_to_all(reply, ('lat', 'lev'), split_axis=1, concat_axis=1, tiled=...  26.2 us
    dynamic_update_slice x32, local copies, waits for them, and re-layouts, legendre_table(): lax.scan(advance, (zeros, zeros, zeros), jnp.arange(degree_total, dtype=j...  25.3 us
    slice x32, local copies, waits for them, and re-layouts, legendre_table(): lax.scan(advance, (zeros, zeros, zeros), jnp.arange(degree_total, dtype=j...  19.7 us
    all_to_all x1, blocking collectives, per_device(): lax.all_to_all(jnp.transpose(grid_grad, (0, 2, 1)).astype(jnp.bfloat16),...  15.5 us
  transfers between devices with their start and end apart: 5, of which 1 were waited for; matrix products, arithmetic and copies ran while one was open for 16% of the time, Pallas kernels for 0%

commit v1 on v0

--- a/solution.py
+++ b/solution.py
@@ -248,8 +248,11 @@
         tiled=True,
     ).astype(jnp.float32)
     coeff_grad = jnp.einsum("jlx,cmx->clmj", grad_rows, dft_table, precision=highest)
-    coeff_grad = lax.all_to_all(
-        shortened(coeff_grad), "lat", split_axis=2, concat_axis=3, tiled=True
+    coeff_grad = jnp.concatenate(
+        lax.all_to_all(
+            jnp.stack(jnp.split(shortened(coeff_grad), lax.axis_size("lat"), axis=2)), "lat", 0, 0
+        ),
+        axis=3,
     ).astype(coeff_grad.dtype)
     spectral_grad = jnp.einsum("nmj,clmj->clmn", legendre, coeff_grad, precision=highest)
     return (spectral_grad, grid_grad)

time: 658 us -> 665 us (1.011)
    unnamed x45 -> x56, local copies, waits for them, and re-layouts: 28.7 us -> 34.1 us
where the time goes in v1:
time: 665 us; the launch traced here: 653 us
  local copies, waits for them, and re-layouts  175 us (26%)
  loops' own time  167 us (25%)
  blocking collectives  125 us (19%)
  other arithmetic  85 us (13%)
  matrix products  54.6 us (8%)
  starting transfers between devices  33.7 us (5%)
  waiting for transfers between devices  8.56 us (1%)
    another operation x1, loops' own time, legendre_table(): lax.scan(advance, (zeros, zeros, zeros), jnp.arange(degree_total, dtype=j...  167 us
    unnamed x1, blocking collectives  69.5 us
    unnamed x56, local copies, waits for them, and re-layouts  34.1 us
    while x224, other arithmetic  31.7 us
    all_to_all x1, blocking collectives, route_back(): lax.all_to_all(reply, ('lat', 'lev'), split_axis=1, concat_axis=1, tiled=...  26.3 us
    dynamic_update_slice x32, local copies, waits for them, and re-layouts, legendre_table(): lax.scan(advance, (zeros, zeros, zeros), jnp.arange(degree_total, dtype=j...  25.3 us
    slice x32, local copies, waits for them, and re-layouts, legendre_table(): lax.scan(advance, (zeros, zeros, zeros), jnp.arange(degree_total, dtype=j...  19.4 us
    all_to_all x1, blocking collectives, per_device(): lax.all_to_all(jnp.transpose(grid_grad, (0, 2, 1)).astype(jnp.bfloat16),...  15.4 us
  transfers between devices with their start and end apart: 5, of which 1 were waited for; matrix products, arithmetic and copies ran while one was open for 16% of the time, Pallas kernels for 0%

profile of v1, /device:TPU:1, one launch (start us, length us, event | category | flops | bytes accessed | tf_op | source)
XLA Modules:
  0.0 652.9 jit_solution(18408877598687010271)
XLA Ops:
  1.0 261.6 %while.23 = (s32[]{:T(128)}, f32[32,384]{1,0:T(8,128)S(1)}, f32[32,384]{1,0:T(8,128)S(1)}, f32[32,384]{1,0:T(8,128)S(1)}, f32[32,8,32,384]{3,2,1,0:T(8,128)}, /*...) while((s32[]{:T(128)}, f32[32,384]{1,0:T(8,128)S(1)}, ...), condition=%wide.region_6.7_spmd.clone.clone.clone.clone, body=%wide.region_5.6_spmd.clone.clone.clone.clone.sunk | while | flops 3778274 | bytes 3127550 | solution.py:67
  262.5 14.5 %fusion.88 = f32[2,8,32,384]{3,1,0,2:T(8,128)S(1)} fusion(f32[256,32,384]{2,1,0:T(8,128)} %bitcast.253, f32[2,8,32,256]{3,2,1,0:T(8,128)S(1)} %copy-done.6), kind=kOutput, calls=%fused_computation.199 | convolution fusion | flops 603979776 | bytes 13893632
  282.8 5.8 all-to-all-start.1
  289.4 69.5 %all-reduce = s32[128]{0:T(128)S(1)} all-reduce(s32[128]{0:T(128)S(1)} %dynamic-update-slice), channel_id=1, replica_groups=mesh['lat'=8,'lev'=16] {'lat','lev'}, use_global_device_ids=true, to_apply=%add | all-reduce | flops 128 | bytes 1024
  363.5 4.1 sine_multiply_fusion
  367.6 5.0 all-to-all-start
  376.7 3.8 reshape.988
  380.5 5.4 copy.209
  389.0 3.7 convolution_bitcast_fusion
  395.0 5.1 reshape.989
  400.1 7.6 %all-to-all-start.2 = ((f32[16,1,18432]{2,1,0:T(1,128)}), f32[16,1,18432]{2,1,0:T(1,128)S(1)}, u32[]{:S(2)}, u32[]{:S(2)}) async-start(f32[16,1,18432]{2,1,0:T(1,128)} %reshape.989), calls=%async_computation.2 | async-start | bytes 2359296 | tf_op jit(solution)/shard_map/all_to_all | solution.py:213
  412.0 11.2 %dynamic_update_slice.19 = bf16[2176,512]{1,0:T(8,128)(2,1)} dynamic-update-slice(bf16[2176,512]{1,0:T(8,128)(2,1)} %broadcast_in_dim.596, bf16[2048,512]{1,0:T(8,128)(2,1)} %bitcast_select_fusion, s32[]{:T(128)S(6)} %select_n.488, s32[]{:T(128)} %constant.254.clone.1) | dynamic-update-slice | bytes 4194308 | tf_op jit(solution)/shard_map/dynamic_update_slice | solution.py:152
  423.2 4.6 copy.171
  428.4 10.1 %all-to-all-start.4 = ((bf16[17,128,512]{2,0,1:T(8,128)(2,1)}), bf16[17,128,512]{2,0,1:T(8,128)(2,1)}, u32[]{:S(2)}, u32[]{:S(2)}) async-start(bf16[17,128,512]{2,0,1:T(8,128)(2,1)} %copy.171), calls=%async_computation.4 | async-start | bytes 6291456 | tf_op jit(solution)/shard_map/all_to_all | solution.py:114
  439.2 4.8 reduce.6
  447.6 5.1 copy.167
  457.3 6.2 gather_fusion.1
  470.3 8.6 %all-to-all-done.4 = bf16[17,128,512]{2,0,1:T(8,128)(2,1)} async-done(((bf16[17,128,512]{2,0,1:T(8,128)(2,1)}), bf16[17,128,512]{2,0,1:T(8,128)(2,1)}, u32[]{:S(2)}, u32[]{:S(2)}) %all-to-all-start.4) | async-done | bytes 2228256 | tf_op jit(solution)/shard_map/all_to_all | solution.py:114
  478.9 5.3 all-to-all-start.3
  485.6 6.8 %gather_fusion = bf16[1024]{0:T(1024)(128)(2,1)S(1)} fusion(bf16[2176]{0:T(1024)(128)(2,1)S(1)} %bitcast.251, s32[1024]{0:T(1024)S(1)} %broadcast_clamp_fusion.1), kind=kCustom, calls=%fused_computation | custom fusion | bytes 8192 | tf_op jit(solution)/shard_map/jit(_take)/gather | solution.py:168
  492.4 4.0 copy.172
  496.5 7.0 %gather_fusion.3 = bf16[1024,512]{1,0:T(8,128)(2,1)} fusion(bf16[2176,512]{1,0:T(8,128)(2,1)} %bitcast.252, s32[1024]{0:T(1024)S(1)} %broadcast_clamp_fusion.1), kind=kCustom, calls=%fused_computation.3 | custom fusion | bytes 2101248 | tf_op jit(solution)/shard_map/jit(_take)/gather | solution.py:167
  508.6 4.3 fusion.85
  512.9 8.8 %multiply_convert_fusion.1 = bf16[1024,1024]{1,0:T(8,128)(2,1)} fusion(f32[1024,1024]{1,0:T(8,128)} %fusion.85, bf16[1024,512]{1,0:T(8,128)(2,1)} %param.21, bf16[1024,512]{1,0:T(8,128)(2,1)S(1)} %copy-done.3, f32[512]{0:T(512)S(1)} %copy-done.18, f32[1024]{0:T(1024)S(1)} %get-tuple-element.400, pred[1024]{0:T(1024)(128)(4,1)S(1)} %get-tuple-element.401), kind=kOutput, calls=%fused_computation.185 | convolution fusion | flops 2165833728 | bytes 8395776 | tf_op jit(solution)/shard_map/dot_general | solution.py:102
  521.7 6.0 fusion.97
  527.7 4.8 gather_fusion.4
  534.4 26.3 %all_to_all.83 = bf16[17,128,128]{2,0,1:T(8,128)(2,1)S(1)} all-to-all(bf16[17,128,128]{2,0,1:T(8,128)(2,1)S(1)} %fusion.108), channel_id=1, replica_groups=mesh['lat'=8,'lev'=16] {'lat','lev'}, dimensions={1} | all-to-all | bytes 1114112 | tf_op jit(solution)/shard_map/all_to_all | solution.py:121
  561.6 12.2 %scatter_custom_fusion = f32[2304,128]{1,0:T(8,128)S(1)} fusion(s32[2048]{0:T(1024)} %bitcast.275, f32[]{:T(128)} %constant.260.clone.1, bf16[2176,128]{1,0:T(8,128)(2,1)} %bitcast.271, s32[]{:T(128)S(6)} %select_n.488, s32[]{:T(128)} %constant.254.clone.1, pred[2048]{0:T(1024)(128)(4,1)S(1)} %copy-done.14, bf16[]{:T(256)} %constant.276.clone.1), kind=kCustom, calls=%fused_computation.208 | custom fusion | flops 786432 | bytes 1707524 | tf_op jit(solution)/shard_map/scatter-add | solution.py:240
  577.5 4.2 reshape.991
  581.6 15.4 %all_to_all.84 = bf16[16,2,9216]{2,1,0:T(2,128)(2,1)} all-to-all(bf16[16,2,9216]{2,1,0:T(2,128)(2,1)} %reshape.991), channel_id=1, replica_groups=mesh['lat'=8,'lev'=16] {'lev'}, dimensions={0} | all-to-all | bytes 1179648 | tf_op jit(solution)/shard_map/all_to_all | solution.py:243
  618.7 13.3 %all_to_all.85 = bf16[8,2,12288]{2,1,0:T(2,128)(2,1)} all-to-all(bf16[8,2,12288]{2,1,0:T(2,128)(2,1)S(1)} %reshape.993), channel_id=1, replica_groups=mesh['lat'=8,'lev'=16] {'lat'}, dimensions={0} | all-to-all | bytes 786432 | tf_op jit(solution)/shard_map/all_to_all | solution.py:252
  638.0 13.3 %fusion.93 = f32[2,8,32,256]{3,1,0,2:T(8,128)S(1)} fusion(bf16[2,8,32,384]{3,1,0,2:T(8,128)(2,1)S(1)} %reshape.978, f32[256,32,384,1]{2,1,0,3:T(8,128)} %bitcast.254), kind=kOutput, calls=%fused_computation.202 | convolution fusion | flops 603979776 | bytes 13500416 | tf_op jit(solution)/shard_map/nmj,clmj->clmn/dot_general | solution.py:257
  (1213 shorter events, 174.5 us)
Async XLA Ops:
  0.6 507.9 %copy-start = (bf16[1024,1024]{1,0:T(8,128)(2,1)S(1)}, bf16[1024,1024]{1,0:T(8,128)(2,1)}, u32[]{:S(2)}) copy-start(bf16[1024,1024]{1,0:T(8,128)(2,1)} %param.20) | copy-start | bytes 6291460
  1.0 261.6 %copy-start.6 = (f32[2,8,32,256]{3,2,1,0:T(8,128)S(1)}, f32[2,8,32,256]{3,2,1,0:T(8,128)}, u32[]{:S(2)}) copy-start(f32[2,8,32,256]{3,2,1,0:T(8,128)} %param.12) | copy-start | bytes 1572868
  279.3 82.7 %copy-start.17 = (s32[1,2048]{1,0:T(1,128)S(1)}, s32[1,2048]{1,0:T(1,128)}, u32[]{:S(2)}) copy-start(s32[1,2048]{1,0:T(1,128)} %param.17) | copy-start | bytes 24580
  282.8 84.7 %all-to-all-start.1 = ((f32[8,1,24576]{2,1,0:T(1,128)}), f32[8,1,24576]{2,1,0:T(1,128)S(1)}, u32[]{:S(2)}, u32[]{:S(2)}) async-start(f32[8,1,24576]{2,1,0:T(1,128)} %reshape.987), calls=%async_computation.1 | async-start | bytes 1572864 | tf_op jit(solution)/shard_map/all_to_all | solution.py:210
  367.6 32.6 %all-to-all-start = ((bf16[17,128,1]{0,2,1:T(2,128)(2,1)}), bf16[17,128,1]{0,2,1:T(2,128)(2,1)S(1)}, u32[]{:S(2)}, u32[]{:S(2)}) async-start(bf16[17,128,1]{0,2,1:T(2,128)(2,1)} %copy.159), calls=%async_computation | async-start | bytes 131072 | tf_op jit(solution)/shard_map/all_to_all | solution.py:115
  400.1 28.2 %all-to-all-start.2 = ((f32[16,1,18432]{2,1,0:T(1,128)}), f32[16,1,18432]{2,1,0:T(1,128)S(1)}, u32[]{:S(2)}, u32[]{:S(2)}) async-start(f32[16,1,18432]{2,1,0:T(1,128)} %reshape.989), calls=%async_computation.2 | async-start | bytes 2359296 | tf_op jit(solution)/shard_map/all_to_all | solution.py:213
  407.7 55.7 %copy-start.13 = (pred[2048]{0:T(1024)(128)(4,1)}, pred[2048]{0:T(1024)(128)(4,1)S(1)}, u32[]{:S(2)}) copy-start(pred[2048]{0:T(1024)(128)(4,1)S(1)} %iota_compare_fusion.1) | copy-start | bytes 6148
  428.3 10.2 %copy-start.11 = (s32[1024]{0:T(1024)}, s32[1024]{0:T(1024)S(1)}, u32[]{:S(2)}) copy-start(s32[1024]{0:T(1024)S(1)} %get-tuple-element.361) | copy-start | bytes 12292
  428.3 10.2 %copy-start.9 = (s32[1024]{0:T(1024)}, s32[1024]{0:T(1024)S(1)}, u32[]{:S(2)}) copy-start(s32[1024]{0:T(1024)S(1)} %get-tuple-element.360) | copy-start | bytes 12292
  428.3 10.2 %copy-start.15 = (s32[1,2048]{1,0:T(1,128)S(1)}, s32[1,2048]{1,0:T(1,128)}, u32[]{:S(2)}) copy-start(s32[1,2048]{1,0:T(1,128)} %param.14) | copy-start | bytes 24580
  428.4 50.5 %all-to-all-start.4 = ((bf16[17,128,512]{2,0,1:T(8,128)(2,1)}), bf16[17,128,512]{2,0,1:T(8,128)(2,1)}, u32[]{:S(2)}, u32[]{:S(2)}) async-start(bf16[17,128,512]{2,0,1:T(8,128)(2,1)} %copy.171), calls=%async_computation.4 | async-start | bytes 6291456 | tf_op jit(solution)/shard_map/all_to_all | solution.py:114
  439.2 8.4 %copy-start.16 = (s32[2048,1]{0,1:T(1,128)}, s32[2048,1]{0,1:T(1,128)S(1)}, u32[]{:S(2)}) copy-start(s32[2048,1]{0,1:T(1,128)S(1)} %compare_select_fusion.2) | copy-start | bytes 24580
  452.7 3.2 copy-start.5
  470.3 22.1 %copy-start.10 = (s32[1024]{0:T(1024)S(1)}, s32[1024]{0:T(1024)}, u32[]{:S(2)}) copy-start(s32[1024]{0:T(1024)} %copy-done.9) | copy-start | bytes 12292
  470.3 22.1 %copy-start.12 = (s32[1024]{0:T(1024)S(1)}, s32[1024]{0:T(1024)}, u32[]{:S(2)}) copy-start(s32[1024]{0:T(1024)} %copy-done.11) | copy-start | bytes 12292
  478.9 24.6 %all-to-all-start.3 = ((bf16[17,128,128]{2,0,1:T(8,128)(2,1)}), bf16[17,128,128]{2,0,1:T(8,128)(2,1)S(1)}, u32[]{:S(2)}, u32[]{:S(2)}) async-start(bf16[17,128,128]{2,0,1:T(8,128)(2,1)} %copy.169), calls=%async_computation.3 | async-start | bytes 1572864 | tf_op jit(solution)/shard_map/all_to_all | solution.py:113
  508.6 4.4 copy-start.2
  508.6 4.4 copy-start.3
  508.6 4.3 copy-start.18
  512.9 8.8 %copy-start.7 = (bf16[128,1024]{1,0:T(8,128)(2,1)S(1)}, bf16[128,1024]{1,0:T(8,128)(2,1)}, u32[]{:S(2)}) copy-start(bf16[128,1024]{1,0:T(8,128)(2,1)} %param.19) | copy-start | bytes 786436
  521.7 6.0 copy-start.8
  532.5 29.1 %copy-start.14 = (pred[2048]{0:T(1024)(128)(4,1)S(1)}, pred[2048]{0:T(1024)(128)(4,1)}, u32[]{:S(2)}) copy-start(pred[2048]{0:T(1024)(128)(4,1)} %copy-done.13) | copy-start | bytes 6148
  573.8 7.8 %copy-start.1 = (f32[2304,128]{1,0:T(8,128)}, f32[2304,128]{1,0:T(8,128)S(1)}, u32[]{:S(2)}) copy-start(f32[2304,128]{1,0:T(8,128)S(1)} %scatter_custom_fusion) | copy-start | bytes 3538948
  600.4 6.4 copy-start.4
